TPU v7x, 256 devices: a whole 4x4x8 slice. The times are simulated.
256 devices in a mesh: group: 16 (over y, x), member: 16 (over z, core).
Axes of the slice: x: 4, y: 4, z: 8, core: 2. Of those that a mesh axis runs over, the one named last changes fastest.
Arguments:
- features: bfloat16 [262144, 1024], P(('group', 'member')), may hold values from -6 to 6
- w_self: bfloat16 [1024, 1024], replicated, may hold values from -0.1875 to 0.1875
- w_neigh: bfloat16 [1024, 1024], replicated, may hold values from -0.1875 to 0.1875
- bias: bfloat16 [1024], replicated, may hold values from -3 to 3
- hub_rows: int32 [1536], P(('group', 'member')), may hold values from 0 to 1023
- hub_nbrs: int32 [262144, 8], P(('group', 'member')), may hold values from 0 to 1535
- local_nbrs: int32 [262144, 16], P(('group', 'member')), may hold values from 0 to 1023
- halo_nbrs: int32 [262144, 16], P(('group', 'member')), may hold values from 0 to 2047
- degrees: int32 [3, 262144], P(None, ('group', 'member')), may hold values from 0 to 16, as said below
- send_rows: int32 [256, 16, 128], P(('group', 'member')), may hold values from 0 to 1023
Outputs:
- hidden_out: bfloat16 [262144, 1024], P(('group', 'member'))
Inputs may be any that keep to these rules, and one draw needn't show every extreme that they name: degrees[0] is at least 1 and reaches 16; degrees[1] reaches 8; degrees[2] reaches 16, each in every draw.
All inputs are finite; a program needn't handle non-finite values.
Results may differ from a plain program's by a relative error of at most 0.002.
Values may be sent and summed in bfloat16 or wider, within the bound.
A program may use at most 128 MiB of HBM per device.

v0:
```python
import math
import jax
import jax.numpy as jnp
from jax import lax
from jax.sharding import PartitionSpec as P


def count_table(index_list, valid_mask, total):
    numbers = jnp.arange(total, dtype=jnp.int32)
    tallies = jnp.zeros((index_list.shape[0], total), jnp.float32)
    for slot in range(index_list.shape[1]):
        hits = (index_list[:, slot][:, None] == numbers[None, :]) & valid_mask[:, slot][:, None]
        tallies = tallies + hits.astype(jnp.float32)
    return tallies.astype(jnp.bfloat16)


def block_mean(
    self_features,
    hub_lookup_matrix,
    neighbour_positions,
    local_index_list,
    hub_index_list,
    halo_index_list,
    deg,
):
    klocal = local_index_list.shape[1]
    khub = hub_index_list.shape[1]
    khalo = halo_index_list.shape[1]
    local_valid_mask = jnp.arange(klocal)[None, :] < deg[0][:, None]
    hub_valid_mask = jnp.arange(khub)[None, :] < deg[1][:, None]
    halo_valid_mask = jnp.arange(khalo)[None, :] < deg[2][:, None]
    local_counts = count_table(local_index_list, local_valid_mask, self_features.shape[0])
    neighbour_sum = jnp.dot(local_counts, self_features, preferred_element_type=jnp.float32)
    hub_counts = count_table(hub_index_list, hub_valid_mask, hub_lookup_matrix.shape[0])
    neighbour_sum = neighbour_sum + jnp.dot(
        hub_counts, hub_lookup_matrix, preferred_element_type=jnp.float32
    )
    halo_counts = count_table(halo_index_list, halo_valid_mask, neighbour_positions.shape[0])
    neighbour_sum = neighbour_sum + jnp.dot(
        halo_counts, neighbour_positions, preferred_element_type=jnp.float32
    )
    count = (
        jnp.sum(local_valid_mask.astype(jnp.float32), axis=1)
        + jnp.sum(hub_valid_mask.astype(jnp.float32), axis=1)
        + jnp.sum(halo_valid_mask.astype(jnp.float32), axis=1)
    )
    return (neighbour_sum / count[:, None]).astype(jnp.bfloat16)


def per_device(
    features, w_self, w_neigh, bias, hub_rows, hub_nbrs, local_nbrs, halo_nbrs, degrees, send_rows
):
    rows_here = features.shape[0]
    width = features.shape[1]
    peers = send_rows.shape[1]
    caps = send_rows.shape[2]
    mine = jnp.take(features, hub_rows, axis=0)
    hub_lookup_matrix = lax.all_gather(mine, ("group", "member"), axis=0, tiled=True)
    outgoing = jnp.take(features, send_rows.reshape(peers * caps), axis=0).reshape(
        peers, caps, width
    )
    received = lax.all_to_all(outgoing, "member", split_axis=0, concat_axis=0, tiled=True)
    neighbour_positions = received.reshape(peers * caps, width)
    blk = math.gcd(rows_here, 256)
    nblocks = rows_here // blk
    local_index_list = local_nbrs.reshape(nblocks, blk, local_nbrs.shape[1])
    hub_index_list = hub_nbrs.reshape(nblocks, blk, hub_nbrs.shape[1])
    halo_index_list = halo_nbrs.reshape(nblocks, blk, halo_nbrs.shape[1])
    deg = degrees.reshape(3, nblocks, blk).transpose(1, 0, 2)

    def one(item):
        return block_mean(
            features, hub_lookup_matrix, neighbour_positions, item[0], item[1], item[2], item[3]
        )

    neigh_mean = lax.map(one, (local_index_list, hub_index_list, halo_index_list, deg)).reshape(
        rows_here, width
    )
    value = jnp.dot(features, w_self, preferred_element_type=jnp.float32)
    value = value + jnp.dot(neigh_mean, w_neigh, preferred_element_type=jnp.float32)
    value = value + bias.astype(jnp.float32)[None, :]
    return jnp.maximum(value, 0.0).astype(jnp.bfloat16)


def solution(mesh):
    in_specs = (
        P(("group", "member"), None),
        P(),
        P(),
        P(),
        P(("group", "member")),
        P(("group", "member"), None),
        P(("group", "member"), None),
        P(("group", "member"), None),
        P(None, ("group", "member")),
        P(("group", "member"), None, None),
    )
    out_specs = P(("group", "member"), None)
    return jax.shard_map(
        per_device, mesh=mesh, in_specs=in_specs, out_specs=out_specs, check_vma=False
    )
```

profile of v0, /device:TPU:1, one launch (start us, length us, event | category | flops | bytes accessed | tf_op | source)
XLA Modules:
  0.0 296.7 jit_solution(11345397366022526329)
XLA Ops:
  6.5 0.0 copy-start
  6.5 0.9 compare_and_fusion
  7.4 0.7 compare_select_fusion
  8.1 12.9 %gather_fusion.1 = bf16[2048,1024]{1,0:T(8,128)(2,1)} fusion(bf16[1024,1024]{1,0:T(8,128)(2,1)} %param.12, s32[2048]{0:T(1024)S(1)} %broadcast_clamp_fusion), kind=kCustom, calls=%fused_computation.1 | custom fusion | bytes 8396800 | tf_op jit(solution)/shard_map/jit(_take)/gather | solution.py:59
  21.0 3.8 %broadcast_select_fusion = bf16[16,128,1024]{2,1,0:T(8,128)(2,1)} fusion(bf16[16,128,1024]{2,1,0:T(8,128)(2,1)} %bitcast.181, pred[16,128]{1,0:T(8,128)(4,1)S(1)} %compare_and_fusion), kind=kLoop, calls=%fused_computation.229 | loop fusion | flops 2097152 | bytes 8390656 | tf_op jit(solution)/shard_map/jit(_take)/select_n | solution.py:59
  24.8 0.0 copy-start.5
  24.8 0.0 copy-start.2
  24.8 0.0 copy-start.3
  24.8 0.0 copy-start.4
  24.8 10.1 %all-to-all-start = ((bf16[16,128,1024]{2,1,0:T(8,128)(2,1)}), bf16[16,128,1024]{2,1,0:T(8,128)(2,1)}, u32[]{:S(2)}, u32[]{:S(2)}) async-start(bf16[16,128,1024]{2,1,0:T(8,128)(2,1)} %broadcast_select_fusion), calls=%async_computation | async-start | bytes 8388608 | tf_op jit(solution)/shard_map/all_to_all | solution.py:62
  34.9 0.0 all-gather.3.cloned.1.call-start
  35.0 0.0 copy-done.5
  35.0 2.4 gather_fusion
  37.5 0.7 select_bitcast_fusion
  38.2 0.0 all-gather.3.cloned.1.call-update
  38.2 0.0 copy-done.2
  38.2 0.0 copy-done.3
  38.3 0.0 copy-done.4
  38.3 0.0 copy-done
  38.3 5.9 %fusion.130 = f32[1024,1024]{1,0:T(8,128)} fusion(bf16[1024,1024]{1,0:T(8,128)(2,1)} %param.12, bf16[1024,1024]{1,0:T(8,128)(2,1)S(1)} %copy-done), kind=kOutput, calls=%fused_computation.241 | convolution fusion | flops 2147483648 | bytes 8388608 | tf_op jit(solution)/shard_map/dot_general | solution.py:79
  44.2 141.6 %all-gather.3.cloned.1.call-done = bf16[256,6,1024]{2,1,0:T(8,128)(2,1)} async-done(((bf16[1,6,1024]{2,1,0:T(8,128)(2,1)}), bf16[256,6,1024]{2,1,0:T(8,128)(2,1)}) %all-gather.3.cloned.1.call-update) | async-done | bytes 3145744 | tf_op jit(solution)/shard_map/all_gather | solution.py:58
  185.8 6.3 %reshape.113 = bf16[1536,1024]{1,0:T(8,128)(2,1)} reshape(bf16[256,6,1024]{2,1,0:T(8,128)(2,1)} %all-gather.3.cloned.1.call-done) | data formatting | bytes 6291456
  192.1 0.0 all-to-all-done
  192.1 90.6 %while.10 = (s32[]{:T(128)}, bf16[4,256,1024]{2,1,0:T(8,128)(2,1)}, s32[4,256,16]{1,0,2:T(4,128)S(1)}, s32[4,3,256]{2,1,0:T(4,128)}, bf16[1024,1024]{1,0:T(8,128...) while((s32[]{:T(128)}, bf16[4,256,1024]{2,1,0:T(8,128)(2,1)}, ...), condition=%wide.region_4.5_spmd, body=%wide.region_0.4_spmd.sunk | while | flops 2479922944 | bytes 22876868 | solution.py:76
  192.1 0.8 constant_dynamic-slice_fusion.8
  193.0 0.7 dynamic-slice_bitcast_fusion.2
  193.7 5.0 %fusion.153 = f32[256,1024]{1,0:T(8,128)S(1)} fusion(bf16[1536,1024]{1,0:T(8,128)(2,1)} %get-tuple-element.437, s32[256]{0:T(256)S(1)} %bitcast.226, s32[256]{0:T(256)S(1)} %bitcast.227, s32[256]{0:T(256)S(1)} %bitcast.228, s32[256]{0:T(256)S(1)} %bitcast.229, s32[256]{0:T(256)S(1)} %bitcast.230, s32[256]{0:T(256)S(1)} %bitcast.231, ...), kind=kOutput, calls=%fused_computation.124.clone.1 | convolution fusion | flops 817889280 | bytes 4204544 | tf_op jit(solution)/shard_map/while/body/eval_jaxpr/dot_general | solution.py:35
  198.8 0.1 slice_reduce_fusion.43
  198.9 0.0 copy-start.1
  198.9 9.7 %fusion.151 = f32[256,1024]{1,0:T(8,128)S(1)} fusion(bf16[2048,1024]{1,0:T(8,128)(2,1)} %get-tuple-element.439, s32[256]{0:T(256)S(1)} %bitcast.210, s32[256]{0:T(256)S(1)} %bitcast.211, s32[256]{0:T(256)S(1)} %bitcast.212, s32[256]{0:T(256)S(1)} %bitcast.213, s32[256]{0:T(256)S(1)} %bitcast.214, s32[256]{0:T(256)S(1)} %bitcast.215, ...), kind=kOutput, calls=%fused_computation.58.clone.1 | convolution fusion | flops 1107296256 | bytes 5263360 | tf_op jit(solution)/shard_map/while/body/eval_jaxpr/dot_general | solution.py:39
  208.7 0.1 slice_reduce_fusion.45
  208.8 0.0 copy-done.1
  208.8 6.0 %fusion.155 = bf16[4,256,1024]{2,1,0:T(8,128)(2,1)} fusion(bf16[4,256,1024]{2,1,0:T(8,128)(2,1)} %get-tuple-element.419, s32[]{:T(128)} %get-tuple-element.418, f32[256,1024]{1,0:T(8,128)S(1)} %fusion.151, f32[256,1024]{1,0:T(8,128)S(1)} %fusion.153, bf16[1024,1024]{1,0:T(8,128)(2,1)S(1)} %copy-done.1, f32[256]{0:T(256)S(1)} %add_add_fusion.2, ...), kind=kOutput, calls=%fused_computation.57.clone.1 | convolution fusion | flops 554696704 | bytes 4740608 | tf_op jit(solution)/shard_map/while/body/eval_jaxpr/dot_general | solution.py:33
  214.8 0.8 constant_dynamic-slice_fusion.8
  215.6 0.7 dynamic-slice_bitcast_fusion.2
  216.4 5.0 %fusion.153 = f32[256,1024]{1,0:T(8,128)S(1)} fusion(bf16[1536,1024]{1,0:T(8,128)(2,1)} %get-tuple-element.437, s32[256]{0:T(256)S(1)} %bitcast.226, s32[256]{0:T(256)S(1)} %bitcast.227, s32[256]{0:T(256)S(1)} %bitcast.228, s32[256]{0:T(256)S(1)} %bitcast.229, s32[256]{0:T(256)S(1)} %bitcast.230, s32[256]{0:T(256)S(1)} %bitcast.231, ...), kind=kOutput, calls=%fused_computation.124.clone.1 | convolution fusion | flops 817889280 | bytes 4204544 | tf_op jit(solution)/shard_map/while/body/eval_jaxpr/dot_general | solution.py:35
  221.4 0.1 slice_reduce_fusion.43
  221.5 0.0 copy-start.1
  221.6 9.7 %fusion.151 = f32[256,1024]{1,0:T(8,128)S(1)} fusion(bf16[2048,1024]{1,0:T(8,128)(2,1)} %get-tuple-element.439, s32[256]{0:T(256)S(1)} %bitcast.210, s32[256]{0:T(256)S(1)} %bitcast.211, s32[256]{0:T(256)S(1)} %bitcast.212, s32[256]{0:T(256)S(1)} %bitcast.213, s32[256]{0:T(256)S(1)} %bitcast.214, s32[256]{0:T(256)S(1)} %bitcast.215, ...), kind=kOutput, calls=%fused_computation.58.clone.1 | convolution fusion | flops 1107296256 | bytes 5263360 | tf_op jit(solution)/shard_map/while/body/eval_jaxpr/dot_general | solution.py:39
  231.3 0.1 slice_reduce_fusion.45
  231.4 0.0 copy-done.1
  231.5 6.0 %fusion.155 = bf16[4,256,1024]{2,1,0:T(8,128)(2,1)} fusion(bf16[4,256,1024]{2,1,0:T(8,128)(2,1)} %get-tuple-element.419, s32[]{:T(128)} %get-tuple-element.418, f32[256,1024]{1,0:T(8,128)S(1)} %fusion.151, f32[256,1024]{1,0:T(8,128)S(1)} %fusion.153, bf16[1024,1024]{1,0:T(8,128)(2,1)S(1)} %copy-done.1, f32[256]{0:T(256)S(1)} %add_add_fusion.2, ...), kind=kOutput, calls=%fused_computation.57.clone.1 | convolution fusion | flops 554696704 | bytes 4740608 | tf_op jit(solution)/shard_map/while/body/eval_jaxpr/dot_general | solution.py:33
  237.4 0.8 constant_dynamic-slice_fusion.8
  238.3 0.7 dynamic-slice_bitcast_fusion.2
  239.0 5.0 %fusion.153 = f32[256,1024]{1,0:T(8,128)S(1)} fusion(bf16[1536,1024]{1,0:T(8,128)(2,1)} %get-tuple-element.437, s32[256]{0:T(256)S(1)} %bitcast.226, s32[256]{0:T(256)S(1)} %bitcast.227, s32[256]{0:T(256)S(1)} %bitcast.228, s32[256]{0:T(256)S(1)} %bitcast.229, s32[256]{0:T(256)S(1)} %bitcast.230, s32[256]{0:T(256)S(1)} %bitcast.231, ...), kind=kOutput, calls=%fused_computation.124.clone.1 | convolution fusion | flops 817889280 | bytes 4204544 | tf_op jit(solution)/shard_map/while/body/eval_jaxpr/dot_general | solution.py:35
  244.0 0.1 slice_reduce_fusion.43
  244.2 0.0 copy-start.1
  244.2 9.7 %fusion.151 = f32[256,1024]{1,0:T(8,128)S(1)} fusion(bf16[2048,1024]{1,0:T(8,128)(2,1)} %get-tuple-element.439, s32[256]{0:T(256)S(1)} %bitcast.210, s32[256]{0:T(256)S(1)} %bitcast.211, s32[256]{0:T(256)S(1)} %bitcast.212, s32[256]{0:T(256)S(1)} %bitcast.213, s32[256]{0:T(256)S(1)} %bitcast.214, s32[256]{0:T(256)S(1)} %bitcast.215, ...), kind=kOutput, calls=%fused_computation.58.clone.1 | convolution fusion | flops 1107296256 | bytes 5263360 | tf_op jit(solution)/shard_map/while/body/eval_jaxpr/dot_general | solution.py:39
  254.0 0.1 slice_reduce_fusion.45
  254.1 0.0 copy-done.1
  254.1 6.0 %fusion.155 = bf16[4,256,1024]{2,1,0:T(8,128)(2,1)} fusion(bf16[4,256,1024]{2,1,0:T(8,128)(2,1)} %get-tuple-element.419, s32[]{:T(128)} %get-tuple-element.418, f32[256,1024]{1,0:T(8,128)S(1)} %fusion.151, f32[256,1024]{1,0:T(8,128)S(1)} %fusion.153, bf16[1024,1024]{1,0:T(8,128)(2,1)S(1)} %copy-done.1, f32[256]{0:T(256)S(1)} %add_add_fusion.2, ...), kind=kOutput, calls=%fused_computation.57.clone.1 | convolution fusion | flops 554696704 | bytes 4740608 | tf_op jit(solution)/shard_map/while/body/eval_jaxpr/dot_general | solution.py:33
  260.1 0.8 constant_dynamic-slice_fusion.8
  260.9 0.7 dynamic-slice_bitcast_fusion.2
  261.7 5.0 %fusion.153 = f32[256,1024]{1,0:T(8,128)S(1)} fusion(bf16[1536,1024]{1,0:T(8,128)(2,1)} %get-tuple-element.437, s32[256]{0:T(256)S(1)} %bitcast.226, s32[256]{0:T(256)S(1)} %bitcast.227, s32[256]{0:T(256)S(1)} %bitcast.228, s32[256]{0:T(256)S(1)} %bitcast.229, s32[256]{0:T(256)S(1)} %bitcast.230, s32[256]{0:T(256)S(1)} %bitcast.231, ...), kind=kOutput, calls=%fused_computation.124.clone.1 | convolution fusion | flops 817889280 | bytes 4204544 | tf_op jit(solution)/shard_map/while/body/eval_jaxpr/dot_general | solution.py:35
  266.7 0.1 slice_reduce_fusion.43
  266.8 0.0 copy-start.1
  266.8 9.7 %fusion.151 = f32[256,1024]{1,0:T(8,128)S(1)} fusion(bf16[2048,1024]{1,0:T(8,128)(2,1)} %get-tuple-element.439, s32[256]{0:T(256)S(1)} %bitcast.210, s32[256]{0:T(256)S(1)} %bitcast.211, s32[256]{0:T(256)S(1)} %bitcast.212, s32[256]{0:T(256)S(1)} %bitcast.213, s32[256]{0:T(256)S(1)} %bitcast.214, s32[256]{0:T(256)S(1)} %bitcast.215, ...), kind=kOutput, calls=%fused_computation.58.clone.1 | convolution fusion | flops 1107296256 | bytes 5263360 | tf_op jit(solution)/shard_map/while/body/eval_jaxpr/dot_general | solution.py:39
  276.6 0.1 slice_reduce_fusion.45
  276.7 0.0 copy-done.1
  276.7 6.0 %fusion.155 = bf16[4,256,1024]{2,1,0:T(8,128)(2,1)} fusion(bf16[4,256,1024]{2,1,0:T(8,128)(2,1)} %get-tuple-element.419, s32[]{:T(128)} %get-tuple-element.418, f32[256,1024]{1,0:T(8,128)S(1)} %fusion.151, f32[256,1024]{1,0:T(8,128)S(1)} %fusion.153, bf16[1024,1024]{1,0:T(8,128)(2,1)S(1)} %copy-done.1, f32[256]{0:T(256)S(1)} %add_add_fusion.2, ...), kind=kOutput, calls=%fused_computation.57.clone.1 | convolution fusion | flops 554696704 | bytes 4740608 | tf_op jit(solution)/shard_map/while/body/eval_jaxpr/dot_general | solution.py:33
  282.7 7.1 %maximum_convert_fusion = bf16[1024,1024]{1,0:T(8,128)(2,1)} fusion(f32[1024,1024]{1,0:T(8,128)} %fusion.130, f32[1024]{0:T(1024)S(1)} %convert_element_type.147, bf16[1024,1024]{1,0:T(8,128)(2,1)} %bitcast.56, bf16[1024,1024]{1,0:T(8,128)(2,1)} %param.14), kind=kOutput, calls=%fused_computation.228 | convolution fusion | flops 2151677952 | bytes 10489856 | tf_op jit(solution)/shard_map/dot_general | solution.py:80
  (60 shorter events, 0.9 us)
Async XLA Ops:
  6.5 31.8 %copy-start = (bf16[1024,1024]{1,0:T(8,128)(2,1)S(1)}, bf16[1024,1024]{1,0:T(8,128)(2,1)}, u32[]{:S(2)}) copy-start(bf16[1024,1024]{1,0:T(8,128)(2,1)} %param.13) | copy-start | bytes 6291460
  24.8 10.2 %copy-start.5 = (s32[6]{0:T(128)S(1)}, s32[6]{0:T(128)}, u32[]{:S(2)}) copy-start(s32[6]{0:T(128)} %param.16) | copy-start | bytes 76
  24.8 13.4 %copy-start.2 = (s32[1024,16]{0,1:T(8,128)S(1)}, s32[1024,16]{0,1:T(8,128)}, u32[]{:S(2)}) copy-start(s32[1024,16]{0,1:T(8,128)} %param.18) | copy-start | bytes 196612
  24.8 13.4 %copy-start.3 = (s32[1024,16]{0,1:T(8,128)S(1)}, s32[1024,16]{0,1:T(8,128)}, u32[]{:S(2)}) copy-start(s32[1024,16]{0,1:T(8,128)} %param.19) | copy-start | bytes 196612
  24.8 13.5 %copy-start.4 = (bf16[1024]{0:T(1024)(128)(2,1)S(1)}, bf16[1024]{0:T(1024)(128)(2,1)}, u32[]{:S(2)}) copy-start(bf16[1024]{0:T(1024)(128)(2,1)} %param.15) | copy-start | bytes 6148
  24.8 167.3 %all-to-all-start = ((bf16[16,128,1024]{2,1,0:T(8,128)(2,1)}), bf16[16,128,1024]{2,1,0:T(8,128)(2,1)}, u32[]{:S(2)}, u32[]{:S(2)}) async-start(bf16[16,128,1024]{2,1,0:T(8,128)(2,1)} %broadcast_select_fusion), calls=%async_computation | async-start | bytes 8388608 | tf_op jit(solution)/shard_map/all_to_all | solution.py:62
  34.9 150.9 %all-gather.3.cloned.1.call-start = ((), (), s32[]{:S(2)}) async-start(), calls=%async_computation.1 | async-start | bytes 4210688 | tf_op jit(solution)/shard_map/all_gather | solution.py:58
  198.9 9.9 %copy-start.1 = (bf16[1024,1024]{1,0:T(8,128)(2,1)S(1)}, bf16[1024,1024]{1,0:T(8,128)(2,1)}, u32[]{:S(2)}) copy-start(bf16[1024,1024]{1,0:T(8,128)(2,1)} %get-tuple-element.435) | copy-start | bytes 6291460 | tf_op jit(solution)/shard_map/while
  221.5 9.9 %copy-start.1 = (bf16[1024,1024]{1,0:T(8,128)(2,1)S(1)}, bf16[1024,1024]{1,0:T(8,128)(2,1)}, u32[]{:S(2)}) copy-start(bf16[1024,1024]{1,0:T(8,128)(2,1)} %get-tuple-element.435) | copy-start | bytes 6291460 | tf_op jit(solution)/shard_map/while
  244.2 9.9 %copy-start.1 = (bf16[1024,1024]{1,0:T(8,128)(2,1)S(1)}, bf16[1024,1024]{1,0:T(8,128)(2,1)}, u32[]{:S(2)}) copy-start(bf16[1024,1024]{1,0:T(8,128)(2,1)} %get-tuple-element.435) | copy-start | bytes 6291460 | tf_op jit(solution)/shard_map/while
  266.8 9.9 %copy-start.1 = (bf16[1024,1024]{1,0:T(8,128)(2,1)S(1)}, bf16[1024,1024]{1,0:T(8,128)(2,1)}, u32[]{:S(2)}) copy-start(bf16[1024,1024]{1,0:T(8,128)(2,1)} %get-tuple-element.435) | copy-start | bytes 6291460 | tf_op jit(solution)/shard_map/while
Sparse Core Ops, SparseCore 0:
  39.5 146.2 all-gather.2
where the time goes:
time: 298 us; the launch traced here: 297 us
  waiting for transfers between devices  142 us (48%)
  matrix products  95.8 us (32%)
  local copies, waits for them, and re-layouts  28.7 us (10%)
  between operations  13.5 us (5%)
  starting transfers between devices  10.2 us (3%)
  other arithmetic  6.4 us (2%)
    all_gather x1, waiting for transfers between devices, per_device(): lax.all_gather(mine, ('group', 'member'), axis=0, tiled=True)  142 us
    dot_general x4, matrix products, block_mean(): jnp.dot(halo_counts, neighbour_positions, preferred_element_type=jnp.floa...  38.9 us
    dot_general x4, matrix products, block_mean(): jnp.dot(local_counts, self_features, preferred_element_type=jnp.float32)  23.9 us
    dot_general x4, matrix products, block_mean(): jnp.dot(hub_counts, hub_lookup_matrix, preferred_element_type=jnp.float32)  20.1 us
    gather x1, local copies, waits for them, and re-layouts, per_device(): jnp.take(features, send_rows.reshape(peers * caps), axis=0)  12.9 us
    all_to_all x1, starting transfers between devices, per_device(): lax.all_to_all(outgoing, 'member', split_axis=0, concat_axis=0, tiled=True)  10.1 us
    dot_general x1, matrix products, per_device(): jnp.dot(neigh_mean, w_neigh, preferred_element_type=jnp.float32)  7.11 us
    unnamed x11, local copies, waits for them, and re-layouts  6.35 us
  transfers between devices with their start and end apart: 2, of which 1 were waited for; matrix products, arithmetic and copies ran while one was open for 5% of the time, Pallas kernels for 0%

commit v1 on v0

--- a/solution.py
+++ b/solution.py
@@ -55,7 +55,12 @@
     peers = send_rows.shape[1]
     caps = send_rows.shape[2]
     mine = jnp.take(features, hub_rows, axis=0)
-    hub_lookup_matrix = lax.all_gather(mine, ("group", "member"), axis=0, tiled=True)
+    hub_lookup_matrix = jnp.concatenate(
+        lax.all_to_all(
+            jnp.stack([mine] * lax.axis_size(("group", "member"))), ("group", "member"), 0, 0
+        ),
+        axis=0,
+    )
     outgoing = jnp.take(features, send_rows.reshape(peers * caps), axis=0).reshape(
         peers, caps, width
     )

time: 298 us -> 317 us (1.064)
  waiting for transfers between devices: 142 us -> 162 us
  between operations: 13.5 us -> 0.12 us
  starting transfers between devices: 10.2 us -> 21.1 us
    all_gather x1 -> x0, waiting for transfers between devices: 142 us -> none  [per_device(): lax.all_gather(mine, ('group', 'member'), axis=0, tiled=True)]
    all_to_all x0 -> x1, waiting for transfers between devices: none -> 82 us  [per_device(): lax.all_to_all(jnp.stack([mine] * lax.axis_size(('group', 'member'))), ('...]
    all_to_all x1, waiting for transfers between devices: 0.01 us -> 80.1 us  [per_device(): lax.all_to_all(outgoing, 'member', split_axis=0, concat_axis=0, tiled=True)]
    all_to_all x0 -> x1, starting transfers between devices: none -> 16.7 us  [per_device(): lax.all_to_all(jnp.stack([mine] * lax.axis_size(('group', 'member'))), ('...]
    unnamed x11 -> x10, local copies, waits for them, and re-layouts: 6.35 us -> 0.02 us
    reshape x0 -> x1, local copies, waits for them, and re-layouts: none -> 6.34 us  [per_device(): jnp.concatenate(lax.all_to_all(jnp.stack([mine] * lax.axis_size(('group',...]
    all_to_all x1, starting transfers between devices: 10.1 us -> 4.44 us  [per_device(): lax.all_to_all(outgoing, 'member', split_axis=0, concat_axis=0, tiled=True)]
  transfers between devices with their start and end apart: 2 -> 2, of which waited for: 1 -> 2; matrix products, arithmetic and copies ran while one was open for 5% -> 9% of each run, Pallas kernels for 0% -> 0%
where the time goes in v1:
time: 317 us; the launch traced here: 316 us
  waiting for transfers between devices  162 us (51%)
  matrix products  95.8 us (30%)
  local copies, waits for them, and re-layouts  31.2 us (10%)
  starting transfers between devices  21.1 us (7%)
  other arithmetic  5.7 us (2%)
    all_to_all x1, waiting for transfers between devices, per_device(): lax.all_to_all(jnp.stack([mine] * lax.axis_size(('group', 'member'))), ('...  82 us
    all_to_all x1, waiting for transfers between devices, per_device(): lax.all_to_all(outgoing, 'member', split_axis=0, concat_axis=0, tiled=True)  80.1 us
    dot_general x4, matrix products, block_mean(): jnp.dot(halo_counts, neighbour_positions, preferred_element_type=jnp.floa...  38.9 us
    dot_general x4, matrix products, block_mean(): jnp.dot(local_counts, self_features, preferred_element_type=jnp.float32)  23.9 us
    dot_general x4, matrix products, block_mean(): jnp.dot(hub_counts, hub_lookup_matrix, preferred_element_type=jnp.float32)  20.1 us
    all_to_all x1, starting transfers between devices, per_device(): lax.all_to_all(jnp.stack([mine] * lax.axis_size(('group', 'member'))), ('...  16.7 us
    gather x1, local copies, waits for them, and re-layouts, per_device(): jnp.take(features, send_rows.reshape(peers * caps), axis=0)  12.8 us
    dot_general x1, matrix products, per_device(): jnp.dot(neigh_mean, w_neigh, preferred_element_type=jnp.float32)  7.11 us
  transfers between devices with their start and end apart: 2, of which 2 were waited for; matrix products, arithmetic and copies ran while one was open for 9% of the time, Pallas kernels for 0%

profile of v1, /device:TPU:1, one launch (start us, length us, event | category | flops | bytes accessed | tf_op | source)
XLA Modules:
  0.0 316.4 jit_solution(386817550294468013)
XLA Ops:
  0.0 0.0 copy-start
  0.0 0.8 compare_select_fusion.2
  0.8 0.7 compare_and_fusion.1
  1.5 2.4 gather_fusion
  3.9 0.1 broadcast_select_fusion.1
  4.0 2.5 stack.2
  6.5 0.0 copy-start.4
  6.5 16.7 %all-to-all-start = ((bf16[256,6,1024]{2,1,0:T(8,128)(2,1)}), bf16[256,6,1024]{2,1,0:T(8,128)(2,1)}, u32[]{:S(2)}, u32[]{:S(2)}) async-start(bf16[256,6,1024]{2,1,0:T(8,128)(2,1)} %stack.2), calls=%async_computation | async-start | bytes 8388608 | tf_op jit(solution)/shard_map/all_to_all | solution.py:59
  23.1 0.0 copy-done.4
  23.2 12.8 %gather_fusion.1 = bf16[2048,1024]{1,0:T(8,128)(2,1)} fusion(bf16[1024,1024]{1,0:T(8,128)(2,1)} %param.12, s32[2048]{0:T(1024)S(1)} %broadcast_clamp_fusion), kind=kCustom, calls=%fused_computation.1 | custom fusion | bytes 8396800 | tf_op jit(solution)/shard_map/jit(_take)/gather | solution.py:64
  36.0 3.8 %broadcast_select_fusion = bf16[16,128,1024]{2,1,0:T(8,128)(2,1)} fusion(bf16[16,128,1024]{2,1,0:T(8,128)(2,1)} %bitcast.179, pred[16,128]{1,0:T(8,128)(4,1)S(1)} %compare_and_fusion), kind=kLoop, calls=%fused_computation.229 | loop fusion | flops 2097152 | bytes 8390656 | tf_op jit(solution)/shard_map/jit(_take)/select_n | solution.py:64
  39.9 0.0 copy-start.2
  39.9 0.0 copy-start.3
  39.9 0.0 copy-start.5
  39.9 82.0 %all-to-all-done = bf16[256,6,1024]{2,1,0:T(8,128)(2,1)} async-done(((bf16[256,6,1024]{2,1,0:T(8,128)(2,1)}), bf16[256,6,1024]{2,1,0:T(8,128)(2,1)}, u32[]{:S(2)}, u32[]{:S(2)}) %all-to-all-start) | async-done | bytes 3145760 | tf_op jit(solution)/shard_map/all_to_all | solution.py:59
  121.9 4.4 %all-to-all-start.1 = ((bf16[16,128,1024]{2,1,0:T(8,128)(2,1)}), bf16[16,128,1024]{2,1,0:T(8,128)(2,1)}, u32[]{:S(2)}, u32[]{:S(2)}) async-start(bf16[16,128,1024]{2,1,0:T(8,128)(2,1)} %broadcast_select_fusion), calls=%async_computation.1 | async-start | bytes 8388608 | tf_op jit(solution)/shard_map/all_to_all | solution.py:67
  126.4 0.0 copy-done.2
  126.4 0.0 copy-done.3
  126.5 0.0 copy-done.5
  126.5 0.0 copy-done
  126.5 5.8 %fusion.130 = f32[1024,1024]{1,0:T(8,128)} fusion(bf16[1024,1024]{1,0:T(8,128)(2,1)} %param.12, bf16[1024,1024]{1,0:T(8,128)(2,1)S(1)} %copy-done), kind=kOutput, calls=%fused_computation.241 | convolution fusion | flops 2147483648 | bytes 8388608 | tf_op jit(solution)/shard_map/dot_general | solution.py:84
  132.3 6.3 %reshape.101 = bf16[1536,1024]{1,0:T(8,128)(2,1)} reshape(bf16[256,6,1024]{2,1,0:T(8,128)(2,1)} %all-to-all-done) | data formatting | bytes 6291456 | tf_op jit(solution)/shard_map/reshape | solution.py:58
  138.7 80.1 %all-to-all-done.1 = bf16[16,128,1024]{2,1,0:T(8,128)(2,1)} async-done(((bf16[16,128,1024]{2,1,0:T(8,128)(2,1)}), bf16[16,128,1024]{2,1,0:T(8,128)(2,1)}, u32[]{:S(2)}, u32[]{:S(2)}) %all-to-all-start.1) | async-done | bytes 4194336 | tf_op jit(solution)/shard_map/all_to_all | solution.py:67
  218.7 90.6 %while.10 = (s32[]{:T(128)}, bf16[4,256,1024]{2,1,0:T(8,128)(2,1)}, s32[4,256,16]{1,0,2:T(4,128)S(1)}, s32[4,3,256]{2,1,0:T(4,128)}, bf16[1024,1024]{1,0:T(8,128...) while((s32[]{:T(128)}, bf16[4,256,1024]{2,1,0:T(8,128)(2,1)}, ...), condition=%wide.region_4.5_spmd, body=%wide.region_0.4_spmd.sunk | while | flops 2479922944 | bytes 22876868 | solution.py:81
  218.7 0.8 constant_dynamic-slice_fusion.8
  219.6 0.7 dynamic-slice_bitcast_fusion.2
  220.3 5.0 %fusion.153 = f32[256,1024]{1,0:T(8,128)S(1)} fusion(bf16[1536,1024]{1,0:T(8,128)(2,1)} %get-tuple-element.428, s32[256]{0:T(256)S(1)} %bitcast.224, s32[256]{0:T(256)S(1)} %bitcast.225, s32[256]{0:T(256)S(1)} %bitcast.226, s32[256]{0:T(256)S(1)} %bitcast.227, s32[256]{0:T(256)S(1)} %bitcast.228, s32[256]{0:T(256)S(1)} %bitcast.229, ...), kind=kOutput, calls=%fused_computation.124.clone.1 | convolution fusion | flops 817889280 | bytes 4204544 | tf_op jit(solution)/shard_map/while/body/eval_jaxpr/dot_general | solution.py:35
  225.3 0.1 slice_reduce_fusion.43
  225.5 0.0 copy-start.1
  225.5 9.7 %fusion.151 = f32[256,1024]{1,0:T(8,128)S(1)} fusion(bf16[2048,1024]{1,0:T(8,128)(2,1)} %get-tuple-element.430, s32[256]{0:T(256)S(1)} %bitcast.208, s32[256]{0:T(256)S(1)} %bitcast.209, s32[256]{0:T(256)S(1)} %bitcast.210, s32[256]{0:T(256)S(1)} %bitcast.211, s32[256]{0:T(256)S(1)} %bitcast.212, s32[256]{0:T(256)S(1)} %bitcast.213, ...), kind=kOutput, calls=%fused_computation.58.clone.1 | convolution fusion | flops 1107296256 | bytes 5263360 | tf_op jit(solution)/shard_map/while/body/eval_jaxpr/dot_general | solution.py:39
  235.3 0.1 slice_reduce_fusion.45
  235.4 0.0 copy-done.1
  235.4 6.0 %fusion.155 = bf16[4,256,1024]{2,1,0:T(8,128)(2,1)} fusion(bf16[4,256,1024]{2,1,0:T(8,128)(2,1)} %get-tuple-element.410, s32[]{:T(128)} %get-tuple-element.409, f32[256,1024]{1,0:T(8,128)S(1)} %fusion.151, f32[256,1024]{1,0:T(8,128)S(1)} %fusion.153, bf16[1024,1024]{1,0:T(8,128)(2,1)S(1)} %copy-done.1, f32[256]{0:T(256)S(1)} %add_add_fusion.2, ...), kind=kOutput, calls=%fused_computation.57.clone.1 | convolution fusion | flops 554696704 | bytes 4740608 | tf_op jit(solution)/shard_map/while/body/eval_jaxpr/dot_general | solution.py:33
  241.4 0.8 constant_dynamic-slice_fusion.8
  242.2 0.7 dynamic-slice_bitcast_fusion.2
  242.9 5.0 %fusion.153 = f32[256,1024]{1,0:T(8,128)S(1)} fusion(bf16[1536,1024]{1,0:T(8,128)(2,1)} %get-tuple-element.428, s32[256]{0:T(256)S(1)} %bitcast.224, s32[256]{0:T(256)S(1)} %bitcast.225, s32[256]{0:T(256)S(1)} %bitcast.226, s32[256]{0:T(256)S(1)} %bitcast.227, s32[256]{0:T(256)S(1)} %bitcast.228, s32[256]{0:T(256)S(1)} %bitcast.229, ...), kind=kOutput, calls=%fused_computation.124.clone.1 | convolution fusion | flops 817889280 | bytes 4204544 | tf_op jit(solution)/shard_map/while/body/eval_jaxpr/dot_general | solution.py:35
  248.0 0.1 slice_reduce_fusion.43
  248.1 0.0 copy-start.1
  248.1 9.7 %fusion.151 = f32[256,1024]{1,0:T(8,128)S(1)} fusion(bf16[2048,1024]{1,0:T(8,128)(2,1)} %get-tuple-element.430, s32[256]{0:T(256)S(1)} %bitcast.208, s32[256]{0:T(256)S(1)} %bitcast.209, s32[256]{0:T(256)S(1)} %bitcast.210, s32[256]{0:T(256)S(1)} %bitcast.211, s32[256]{0:T(256)S(1)} %bitcast.212, s32[256]{0:T(256)S(1)} %bitcast.213, ...), kind=kOutput, calls=%fused_computation.58.clone.1 | convolution fusion | flops 1107296256 | bytes 5263360 | tf_op jit(solution)/shard_map/while/body/eval_jaxpr/dot_general | solution.py:39
  257.9 0.1 slice_reduce_fusion.45
  258.0 0.0 copy-done.1
  258.0 6.0 %fusion.155 = bf16[4,256,1024]{2,1,0:T(8,128)(2,1)} fusion(bf16[4,256,1024]{2,1,0:T(8,128)(2,1)} %get-tuple-element.410, s32[]{:T(128)} %get-tuple-element.409, f32[256,1024]{1,0:T(8,128)S(1)} %fusion.151, f32[256,1024]{1,0:T(8,128)S(1)} %fusion.153, bf16[1024,1024]{1,0:T(8,128)(2,1)S(1)} %copy-done.1, f32[256]{0:T(256)S(1)} %add_add_fusion.2, ...), kind=kOutput, calls=%fused_computation.57.clone.1 | convolution fusion | flops 554696704 | bytes 4740608 | tf_op jit(solution)/shard_map/while/body/eval_jaxpr/dot_general | solution.py:33
  264.0 0.8 constant_dynamic-slice_fusion.8
  264.9 0.7 dynamic-slice_bitcast_fusion.2
  265.6 5.0 %fusion.153 = f32[256,1024]{1,0:T(8,128)S(1)} fusion(bf16[1536,1024]{1,0:T(8,128)(2,1)} %get-tuple-element.428, s32[256]{0:T(256)S(1)} %bitcast.224, s32[256]{0:T(256)S(1)} %bitcast.225, s32[256]{0:T(256)S(1)} %bitcast.226, s32[256]{0:T(256)S(1)} %bitcast.227, s32[256]{0:T(256)S(1)} %bitcast.228, s32[256]{0:T(256)S(1)} %bitcast.229, ...), kind=kOutput, calls=%fused_computation.124.clone.1 | convolution fusion | flops 817889280 | bytes 4204544 | tf_op jit(solution)/shard_map/while/body/eval_jaxpr/dot_general | solution.py:35
  270.6 0.1 slice_reduce_fusion.43
  270.8 0.0 copy-start.1
  270.8 9.7 %fusion.151 = f32[256,1024]{1,0:T(8,128)S(1)} fusion(bf16[2048,1024]{1,0:T(8,128)(2,1)} %get-tuple-element.430, s32[256]{0:T(256)S(1)} %bitcast.208, s32[256]{0:T(256)S(1)} %bitcast.209, s32[256]{0:T(256)S(1)} %bitcast.210, s32[256]{0:T(256)S(1)} %bitcast.211, s32[256]{0:T(256)S(1)} %bitcast.212, s32[256]{0:T(256)S(1)} %bitcast.213, ...), kind=kOutput, calls=%fused_computation.58.clone.1 | convolution fusion | flops 1107296256 | bytes 5263360 | tf_op jit(solution)/shard_map/while/body/eval_jaxpr/dot_general | solution.py:39
  280.6 0.1 slice_reduce_fusion.45
  280.7 0.0 copy-done.1
  280.7 6.0 %fusion.155 = bf16[4,256,1024]{2,1,0:T(8,128)(2,1)} fusion(bf16[4,256,1024]{2,1,0:T(8,128)(2,1)} %get-tuple-element.410, s32[]{:T(128)} %get-tuple-element.409, f32[256,1024]{1,0:T(8,128)S(1)} %fusion.151, f32[256,1024]{1,0:T(8,128)S(1)} %fusion.153, bf16[1024,1024]{1,0:T(8,128)(2,1)S(1)} %copy-done.1, f32[256]{0:T(256)S(1)} %add_add_fusion.2, ...), kind=kOutput, calls=%fused_computation.57.clone.1 | convolution fusion | flops 554696704 | bytes 4740608 | tf_op jit(solution)/shard_map/while/body/eval_jaxpr/dot_general | solution.py:33
  286.7 0.8 constant_dynamic-slice_fusion.8
  287.5 0.7 dynamic-slice_bitcast_fusion.2
  288.2 5.0 %fusion.153 = f32[256,1024]{1,0:T(8,128)S(1)} fusion(bf16[1536,1024]{1,0:T(8,128)(2,1)} %get-tuple-element.428, s32[256]{0:T(256)S(1)} %bitcast.224, s32[256]{0:T(256)S(1)} %bitcast.225, s32[256]{0:T(256)S(1)} %bitcast.226, s32[256]{0:T(256)S(1)} %bitcast.227, s32[256]{0:T(256)S(1)} %bitcast.228, s32[256]{0:T(256)S(1)} %bitcast.229, ...), kind=kOutput, calls=%fused_computation.124.clone.1 | convolution fusion | flops 817889280 | bytes 4204544 | tf_op jit(solution)/shard_map/while/body/eval_jaxpr/dot_general | solution.py:35
  293.3 0.1 slice_reduce_fusion.43
  293.4 0.0 copy-start.1
  293.4 9.7 %fusion.151 = f32[256,1024]{1,0:T(8,128)S(1)} fusion(bf16[2048,1024]{1,0:T(8,128)(2,1)} %get-tuple-element.430, s32[256]{0:T(256)S(1)} %bitcast.208, s32[256]{0:T(256)S(1)} %bitcast.209, s32[256]{0:T(256)S(1)} %bitcast.210, s32[256]{0:T(256)S(1)} %bitcast.211, s32[256]{0:T(256)S(1)} %bitcast.212, s32[256]{0:T(256)S(1)} %bitcast.213, ...), kind=kOutput, calls=%fused_computation.58.clone.1 | convolution fusion | flops 1107296256 | bytes 5263360 | tf_op jit(solution)/shard_map/while/body/eval_jaxpr/dot_general | solution.py:39
  303.2 0.1 slice_reduce_fusion.45
  303.3 0.0 copy-done.1
  303.3 6.0 %fusion.155 = bf16[4,256,1024]{2,1,0:T(8,128)(2,1)} fusion(bf16[4,256,1024]{2,1,0:T(8,128)(2,1)} %get-tuple-element.410, s32[]{:T(128)} %get-tuple-element.409, f32[256,1024]{1,0:T(8,128)S(1)} %fusion.151, f32[256,1024]{1,0:T(8,128)S(1)} %fusion.153, bf16[1024,1024]{1,0:T(8,128)(2,1)S(1)} %copy-done.1, f32[256]{0:T(256)S(1)} %add_add_fusion.2, ...), kind=kOutput, calls=%fused_computation.57.clone.1 | convolution fusion | flops 554696704 | bytes 4740608 | tf_op jit(solution)/shard_map/while/body/eval_jaxpr/dot_general | solution.py:33
  309.3 7.1 %maximum_convert_fusion = bf16[1024,1024]{1,0:T(8,128)(2,1)} fusion(f32[1024,1024]{1,0:T(8,128)} %fusion.130, f32[1024]{0:T(1024)S(1)} %convert_element_type.147, bf16[1024,1024]{1,0:T(8,128)(2,1)} %bitcast.55, bf16[1024,1024]{1,0:T(8,128)(2,1)} %param.14), kind=kOutput, calls=%fused_computation.228 | convolution fusion | flops 2151677952 | bytes 10489856 | tf_op jit(solution)/shard_map/dot_general | solution.py:85
  (60 shorter events, 0.9 us)
Async XLA Ops:
  0.0 126.5 %copy-start = (bf16[1024,1024]{1,0:T(8,128)(2,1)S(1)}, bf16[1024,1024]{1,0:T(8,128)(2,1)}, u32[]{:S(2)}) copy-start(bf16[1024,1024]{1,0:T(8,128)(2,1)} %param.13) | copy-start | bytes 6291460
  6.5 16.7 %copy-start.4 = (s32[1,16,128]{2,1,0:T(8,128)S(1)}, s32[1,16,128]{2,1,0:T(8,128)}, u32[]{:S(2)}) copy-start(s32[1,16,128]{2,1,0:T(8,128)} %param.21) | copy-start | bytes 24580
  6.5 115.4 %all-to-all-start = ((bf16[256,6,1024]{2,1,0:T(8,128)(2,1)}), bf16[256,6,1024]{2,1,0:T(8,128)(2,1)}, u32[]{:S(2)}, u32[]{:S(2)}) async-start(bf16[256,6,1024]{2,1,0:T(8,128)(2,1)} %stack.2), calls=%async_computation | async-start | bytes 8388608 | tf_op jit(solution)/shard_map/all_to_all | solution.py:59
  39.9 86.5 %copy-start.2 = (s32[1024,16]{0,1:T(8,128)S(1)}, s32[1024,16]{0,1:T(8,128)}, u32[]{:S(2)}) copy-start(s32[1024,16]{0,1:T(8,128)} %param.19) | copy-start | bytes 196612
  39.9 86.6 %copy-start.3 = (s32[1024,16]{0,1:T(8,128)S(1)}, s32[1024,16]{0,1:T(8,128)}, u32[]{:S(2)}) copy-start(s32[1024,16]{0,1:T(8,128)} %param.18) | copy-start | bytes 196612
  39.9 86.6 %copy-start.5 = (bf16[1024]{0:T(1024)(128)(2,1)S(1)}, bf16[1024]{0:T(1024)(128)(2,1)}, u32[]{:S(2)}) copy-start(bf16[1024]{0:T(1024)(128)(2,1)} %param.15) | copy-start | bytes 6148
  121.9 96.8 %all-to-all-start.1 = ((bf16[16,128,1024]{2,1,0:T(8,128)(2,1)}), bf16[16,128,1024]{2,1,0:T(8,128)(2,1)}, u32[]{:S(2)}, u32[]{:S(2)}) async-start(bf16[16,128,1024]{2,1,0:T(8,128)(2,1)} %broadcast_select_fusion), calls=%async_computation.1 | async-start | bytes 8388608 | tf_op jit(solution)/shard_map/all_to_all | solution.py:67
  225.5 9.9 %copy-start.1 = (bf16[1024,1024]{1,0:T(8,128)(2,1)S(1)}, bf16[1024,1024]{1,0:T(8,128)(2,1)}, u32[]{:S(2)}) copy-start(bf16[1024,1024]{1,0:T(8,128)(2,1)} %get-tuple-element.426) | copy-start | bytes 6291460 | tf_op jit(solution)/shard_map/while
  248.1 9.9 %copy-start.1 = (bf16[1024,1024]{1,0:T(8,128)(2,1)S(1)}, bf16[1024,1024]{1,0:T(8,128)(2,1)}, u32[]{:S(2)}) copy-start(bf16[1024,1024]{1,0:T(8,128)(2,1)} %get-tuple-element.426) | copy-start | bytes 6291460 | tf_op jit(solution)/shard_map/while
  270.8 9.9 %copy-start.1 = (bf16[1024,1024]{1,0:T(8,128)(2,1)S(1)}, bf16[1024,1024]{1,0:T(8,128)(2,1)}, u32[]{:S(2)}) copy-start(bf16[1024,1024]{1,0:T(8,128)(2,1)} %get-tuple-element.426) | copy-start | bytes 6291460 | tf_op jit(solution)/shard_map/while
  293.4 9.9 %copy-start.1 = (bf16[1024,1024]{1,0:T(8,128)(2,1)S(1)}, bf16[1024,1024]{1,0:T(8,128)(2,1)}, u32[]{:S(2)}) copy-start(bf16[1024,1024]{1,0:T(8,128)(2,1)} %get-tuple-element.426) | copy-start | bytes 6291460 | tf_op jit(solution)/shard_map/while
